TPU v7x, 32 devices: a whole 2x2x4 slice. The times are simulated.
32 devices in a mesh: grp: 2 (over y), row: 4 (over z), col: 4 (over x, core).
Axes of the slice: x: 2, y: 2, z: 4, core: 2. Of those that a mesh axis runs over, the one named last changes fastest.
Arguments:
- sky_cube: bfloat16 [1024, 512, 512], P(('grp', 'row'), 'col'), parts along dimension 0, may hold values from -40 to 40
- half_widths: int32 [512], replicated, may hold values from 1 to 16, as said below
- pixel_mask: int32 [1024, 512], P(('grp', 'row'), 'col'), parts along dimension 0, may hold values 0 or 1
- foreground_modes: float32 [32, 512], P('grp'), parts along dimension 0, may hold values from -6 to 6
Outputs:
- spectrum: float32 [512, 2, 512, 512], P(('grp', 'row', 'col')), parts along dimension 0
- channel_weights: float32 [1024], P('grp'), parts along dimension 0
There are 2 independent parts, one for each index of `grp`. A program takes and returns all parts, laid end to end along the dimension named above; an argument that names none is the same for every part. Nothing has to cross between parts.
Inputs may be any that keep to these rules, and one draw needn't show every extreme that they name: `half_widths`: some channel has half-width exactly 16 and some exactly 1.
All inputs are finite; a program needn't handle non-finite values. No bound on the sum of `pixel_mask` on one device may be relied on, other than what follows from the above.
Results may differ from a plain program's by a relative error of at most 0.0087.
Values may be sent and summed in bfloat16 or wider, within the bound.
A program may use at most 192 MiB of HBM per device.

v0:
```python
import functools
import math

import jax
import jax.numpy as jnp
from jax import lax
from jax.experimental import pallas as pl
from jax.experimental.pallas import tpu as pltpu
from jax.sharding import PartitionSpec as P

NR = 512
NC = 512
HALF = 16
TAIL = 8


highest = lax.Precision.HIGHEST


def padded(x, sides, width):
    for axis, dim in sides:
        size, length = (lax.axis_size(axis), x.shape[dim])
        up = [(i, (i + 1) % size) for i in range(size - 1)]
        down = [(j, i) for i, j in up]
        last = lax.slice_in_dim(x, length - width, length, axis=dim)
        initial = lax.slice_in_dim(x, 0, width, axis=dim)
        before = lax.ppermute(last, axis, up)
        after = lax.ppermute(initial, axis, down)
        x = jnp.concatenate([before, x, after], axis=dim)
    return x


def make_taps(half_widths):
    offsets = jnp.arange(2 * HALF + 1, dtype=jnp.int32) - HALF
    distance = offsets.astype(jnp.float32)[:, None]
    spread = half_widths.astype(jnp.float32)[None, :] * 0.5
    inside = jnp.abs(offsets)[:, None] <= half_widths[None, :]
    profile = jnp.where(
        inside, jnp.exp(-distance * distance / (2.0 * spread * spread)), jnp.float32(0.0)
    )
    return (profile / jnp.sum(profile, axis=0, keepdims=True)).astype(jnp.bfloat16)


def banded_taps(outputs, beam_taps):
    offsets = (
        jnp.arange(outputs + 2 * HALF, dtype=jnp.int32)[None, :]
        - jnp.arange(outputs, dtype=jnp.int32)[:, None]
    )
    one_hot = (
        offsets[:, :, None] == jnp.arange(2 * HALF + 1, dtype=jnp.int32)[None, None, :]
    ).astype(jnp.bfloat16)
    return jnp.einsum("oit,tf->oif", one_hot, beam_taps, preferred_element_type=jnp.float32).astype(
        jnp.bfloat16
    )


def window_taper(length):
    angles = 2.0 * math.pi * jnp.arange(length, dtype=jnp.int32).astype(jnp.float32) / (length - 1)
    return (
        0.35875
        - 0.48829 * jnp.cos(angles)
        + 0.14128 * jnp.cos(2.0 * angles)
        - 0.01168 * jnp.cos(3.0 * angles)
    )


def dft_table(length):
    indices = jnp.arange(length, dtype=jnp.int32)
    product = indices[:, None] * indices[None, :] % length
    angles = 2.0 * math.pi * product.astype(jnp.float32) / length
    cosine = jnp.cos(angles) / math.sqrt(length)
    sine_part = -jnp.sin(angles) / math.sqrt(length)
    table = jnp.stack([jnp.stack([cosine, -sine_part]), jnp.stack([sine_part, cosine])])
    return table.astype(jnp.bfloat16)


def tile_delay_table(channels, peers):
    per_device = channels // 2 // peers
    slot_index = jnp.arange(channels, dtype=jnp.int32)
    item_index = slot_index // (2 * peers)
    peer_index = slot_index // 2 % peers
    component = slot_index % 2
    delay_index = peer_index * per_device + item_index
    channel_index = jnp.arange(channels, dtype=jnp.int32)
    product = delay_index[:, None] * channel_index[None, :] % channels
    angles = 2.0 * math.pi * product.astype(jnp.float32) / channels
    rows_out = jnp.where(component[:, None] == 0, jnp.cos(angles), -jnp.sin(angles))
    return rows_out * (window_taper(channels) / math.sqrt(channels))[None, :]


def spatial_transform(regrouped):
    items = regrouped.shape[0]
    row_count = lax.axis_size("row")
    col_count = lax.axis_size("col")
    tile_rows = NR // row_count
    tile_cols = NC // col_count
    delay_slab = regrouped.reshape(items, 2, row_count, col_count, tile_rows, tile_cols)
    delay_slab = delay_slab.transpose(0, 1, 2, 4, 3, 5).reshape(items, 2, NR, NC)
    halfway = jnp.einsum(
        "kmrc,nmcd->knrd", delay_slab, dft_table(NC), preferred_element_type=jnp.float32
    )
    halfway = halfway.astype(jnp.bfloat16)
    return jnp.einsum("nmsr,kmrd->knsd", dft_table(NR), halfway, preferred_element_type=jnp.float32)


def body(sky_cube, half_widths, pixel_mask, foreground_modes):
    tile_rows, tile_cols, channels = sky_cube.shape
    beam_taps = make_taps(half_widths)
    row_band = banded_taps(tile_rows, beam_taps)
    extended = padded(sky_cube, (("row", 0),), HALF)
    row_part = jnp.einsum(
        "oif,icf->ocf", row_band, extended, preferred_element_type=jnp.float32
    ).astype(jnp.bfloat16)
    row_smoothed = padded(row_part, (("col", 1),), HALF)
    column_band = banded_taps(tile_cols, beam_taps)
    smoothed = jnp.einsum(
        "oif,rif->rof", column_band, row_smoothed, preferred_element_type=jnp.float32
    )
    masked = pixel_mask.astype(jnp.float32)[:, :, None] * smoothed
    pixels = masked.reshape(tile_rows * tile_cols, channels)
    peers = lax.axis_size("row") * lax.axis_size("col")
    delay_table = tile_delay_table(channels, peers)
    power_sum = lax.psum(jnp.sum(masked * masked, axis=(0, 1)), ("row", "col"))
    weights = 1.0 / (power_sum / (NR * NC) + 1e-05)
    channel_weights = weights / jnp.mean(weights)
    weighted_modes = foreground_modes * weights[None, :]
    normal_matrix = jnp.dot(
        weighted_modes, foreground_modes.T, precision=highest, preferred_element_type=jnp.float32
    )
    projected = jnp.dot(
        pixels, weighted_modes.T, precision=highest, preferred_element_type=jnp.float32
    )
    factor = jnp.linalg.cholesky(normal_matrix)
    amplitude = jax.scipy.linalg.cho_solve((factor, True), projected.T)
    cleaned = pixels - jnp.dot(
        amplitude.T, foreground_modes, precision=highest, preferred_element_type=jnp.float32
    )
    delay_tile = lax.dot_general(
        delay_table,
        cleaned,
        (((1,), (1,)), ((), ())),
        precision=highest,
        preferred_element_type=jnp.float32,
    )
    per_device = channels // 2 // peers
    sendable = delay_tile.astype(jnp.bfloat16).reshape(
        per_device, peers, 2, 1, 1, tile_rows * tile_cols
    )
    spectrum = spatial_transform(
        lax.all_to_all(sendable, ("row", "col"), split_axis=1, concat_axis=3, tiled=True)
    )
    return (spectrum, channel_weights)


FBLOCK = 16
RBLOCK = 16


def band_tables(outputs):
    widths = jnp.arange(1, HALF + 1, dtype=jnp.int32)
    spread = widths.astype(jnp.float32) * 0.5
    offsets = jnp.arange(2 * HALF + 1, dtype=jnp.int32) - HALF

    def profile(t, width, spread):
        d = t.astype(jnp.float32)
        return jnp.where(
            jnp.abs(t) <= width, jnp.exp(-d * d / (2.0 * spread * spread)), jnp.float32(0.0)
        )

    total = jnp.sum(profile(offsets[:, None], widths[None, :], spread[None, :]), axis=0)
    place = jnp.concatenate(
        [
            jnp.arange(outputs, dtype=jnp.int32),
            jnp.arange(HALF, dtype=jnp.int32) - HALF,
            jnp.arange(HALF, dtype=jnp.int32) + outputs,
        ]
    )
    t = place[None, None, :] - jnp.arange(outputs, dtype=jnp.int32)[None, :, None]
    w3, s3, n3 = (v[:, None, None] for v in (widths, spread, total))
    return (profile(t, w3, s3) / n3).astype(jnp.bfloat16)


def smooth_kernel(hw_ref, main_ref, rowh_ref, colh_ref, corner_ref, mask_ref, brow_ref, bcol_ref, out_ref, pow_ref):
    rows, fblock, cols = out_ref.shape
    flat = out_ref.reshape(rows * fblock, cols)
    base = pl.program_id(0) * fblock
    mask = mask_ref[...]
    for i in range(fblock):
        pick = hw_ref[base + i] - 1
        left = jnp.concatenate([main_ref[i], rowh_ref[i]], axis=0)
        right = jnp.concatenate([colh_ref[i], corner_ref[i]], axis=0)
        ext = jnp.concatenate([left, right], axis=1)
        part = jnp.dot(brow_ref[pick], ext, preferred_element_type=jnp.float32).astype(jnp.bfloat16)
        done = jnp.dot(part, bcol_ref[pick], preferred_element_type=jnp.float32) * mask
        flat[pl.ds(i, rows, stride=fblock), :] = done
        pow_ref[pl.ds(i, 1), :] = jnp.sum(done * done, axis=0, keepdims=True)


def smooth(half_widths, main, rowh, colh, corner, mask, brow, bcol):
    channels, rows, cols = main.shape
    step = lambda a: pl.BlockSpec((FBLOCK,) + a.shape[1:], lambda i, hw: (i, 0, 0))
    whole = lambda a: pl.BlockSpec(a.shape, lambda i, hw: (0,) * a.ndim)
    return pl.pallas_call(
        smooth_kernel,
        grid_spec=pltpu.PrefetchScalarGridSpec(
            num_scalar_prefetch=1,
            grid=(channels // FBLOCK,),
            in_specs=[step(main), step(rowh), step(colh), step(corner), whole(mask), whole(brow), whole(bcol)],
            out_specs=[
                pl.BlockSpec((rows, FBLOCK, cols), lambda i, hw: (0, i, 0)),
                pl.BlockSpec((FBLOCK, cols), lambda i, hw: (i, 0)),
            ],
        ),
        out_shape=[
            jax.ShapeDtypeStruct((rows, channels, cols), jnp.float32),
            jax.ShapeDtypeStruct((channels, cols), jnp.float32),
        ],
        name="smooth",
    )(half_widths, main, rowh, colh, corner, mask, brow, bcol)


def split3(x):
    first = x.astype(jnp.bfloat16)
    rest = x - first.astype(jnp.float32)
    second = rest.astype(jnp.bfloat16)
    third = (rest - second.astype(jnp.float32)).astype(jnp.bfloat16)
    return first, second, third


def outer_split3(x):
    first = lax.reduce_precision(x, 8, 7)
    second = lax.reduce_precision(x - first, 8, 7)
    third = lax.reduce_precision(x - first - second, 8, 7)
    return [v.astype(jnp.bfloat16) for v in (first, second, third)]


def delay_kernel(n, masked_ref, fit_ref, modes_ref, table_ref, *refs):
    outs, stage = refs[:n], refs[n]
    rblock, channels, cols = masked_ref.shape
    k = fit_ref.shape[0] // 3
    dot = functools.partial(jnp.dot, preferred_element_type=jnp.float32)

    def pair(j, carry):
        x = jnp.concatenate([masked_ref[2 * j], masked_ref[2 * j + 1]], axis=1)
        x1, x2, x3 = split3(x)
        p1 = dot(fit_ref[...], x1)
        p2 = dot(fit_ref[: 2 * k], x2)
        p3 = dot(fit_ref[:k], x3)
        amp = p1[:k] + ((p1[k : 2 * k] + p2[:k]) + (p1[2 * k :] + p2[k:] + p3))
        a1, a2, a3 = split3(amp)
        stack = jnp.concatenate([a1, a2, a1, a2, a3, a1], axis=0)
        cleaned = (x - dot(modes_ref[...], stack)).astype(jnp.bfloat16)
        delays = dot(table_ref[...], cleaned)
        slots = delays.shape[0]
        stage[pl.ds(2 * j, slots, stride=rblock), :] = delays[:, :cols]
        stage[pl.ds(2 * j + 1, slots, stride=rblock), :] = delays[:, cols:]
        return carry

    lax.fori_loop(0, rblock // 2, pair, 0, unroll=2)
    start = 0
    for out in outs:
        size = math.prod(out.shape[:3])
        out[...] = stage[start : start + size, :].astype(jnp.bfloat16).reshape(out.shape)
        start += size


def clean_delay(masked, fit, modes, table, sizes, peers):
    rows, channels, cols = masked.shape
    whole = lambda a: pl.BlockSpec(a.shape, lambda i: (0,) * a.ndim)
    return pl.pallas_call(
        functools.partial(delay_kernel, len(sizes)),
        grid=(rows // RBLOCK,),
        in_specs=[pl.BlockSpec((RBLOCK, channels, cols), lambda i: (i, 0, 0)), whole(fit), whole(modes), whole(table)],
        out_specs=[pl.BlockSpec((peers, 2 * k, RBLOCK, cols), lambda i: (0, 0, i, 0)) for k in sizes],
        out_shape=[jax.ShapeDtypeStruct((peers, 2 * k, rows, cols), jnp.bfloat16) for k in sizes],
        scratch_shapes=[pltpu.VMEM((table.shape[0] * RBLOCK, cols), jnp.float32)],
        name="clean_delay",
    )(masked, fit, modes, table)


def spatial_kernel(row_count, col_count, inputs, data_ref, ctab_ref, rtab_ref, *refs):
    out_ref = refs[inputs - 3]
    nr, nc = out_ref.shape[2:]
    lines = []
    for i in range(row_count):
        tiles = [data_ref[i * col_count + j, m] for m in range(2) for j in range(col_count)]
        lines.append(jnp.concatenate(tiles, axis=1))
    slab = jnp.concatenate(lines, axis=0)
    half = jnp.dot(slab, ctab_ref[...], preferred_element_type=jnp.float32).astype(jnp.bfloat16)
    half = jnp.concatenate([half[:, :nc], half[:, nc:]], axis=0)
    for m in range(2):
        out_ref[0, m] = jnp.dot(
            rtab_ref[m * nr : (m + 1) * nr, :], half, preferred_element_type=jnp.float32
        )


def spatial(data, ctab, rtab, before, first, total, row_count, col_count):
    peers, slots, rows, cols = data.shape
    items = slots // 2
    whole = lambda a: pl.BlockSpec(a.shape, lambda i: (0,) * a.ndim)
    nr, nc = rtab.shape[0] // 2, ctab.shape[0] // 2
    in_specs = [pl.BlockSpec((peers, 2, rows, cols), lambda i: (0, i, 0, 0)), whole(ctab), whole(rtab)]
    out_specs = [pl.BlockSpec((1, 2, nr, nc), lambda i: (first + i, 0, 0, 0))]
    out_shape = [jax.ShapeDtypeStruct((total, 2, nr, nc), jnp.float32)]
    args = [data, ctab, rtab]
    alias = {}
    if before is not None:
        alias[len(args)] = 0
        in_specs.append(pl.BlockSpec(memory_space=pl.ANY))
        args.append(before)
    out = pl.pallas_call(
        functools.partial(spatial_kernel, row_count, col_count, len(args)),
        grid=(items,),
        in_specs=in_specs,
        out_specs=out_specs,
        out_shape=out_shape,
        input_output_aliases=alias,
        cost_estimate=pl.CostEstimate(
            flops=items * 8 * (nr * nc * nc + nr * nr * nc),
            bytes_accessed=items * nr * nc * 12,
            transcendentals=0,
        ),
        name="spatial",
    )(*args)
    return out[0]


def halo(x, axis, dim):
    size, length = lax.axis_size(axis), x.shape[dim]
    up = [(i, (i + 1) % size) for i in range(size - 1)]
    down = [(j, i) for i, j in up]
    before = lax.ppermute(lax.slice_in_dim(x, length - HALF, length, axis=dim), axis, up)
    after = lax.ppermute(lax.slice_in_dim(x, 0, HALF, axis=dim), axis, down)
    return jnp.concatenate([before, after], axis=dim)


def chunked_delay_table(channels, peers, sizes):
    per_device = channels // 2 // peers
    delays, first = [], 0
    for size in sizes:
        slot = jnp.arange(2 * size * peers, dtype=jnp.int32)
        delays.append(slot // (2 * size) * per_device + first + slot // 2 % size)
        first += size
    delay = jnp.concatenate(delays)
    component = jnp.arange(channels, dtype=jnp.int32) % 2
    product = delay[:, None] * jnp.arange(channels, dtype=jnp.int32)[None, :] % channels
    angles = 2.0 * math.pi * product.astype(jnp.float32) / channels
    rows_out = jnp.where(component[:, None] == 0, jnp.cos(angles), -jnp.sin(angles))
    return (rows_out * (window_taper(channels) / math.sqrt(channels))[None, :]).astype(jnp.bfloat16)


def tiled_body(sky_cube, half_widths, pixel_mask, foreground_modes):
    tile_rows, tile_cols, channels = sky_cube.shape
    row_count, col_count = lax.axis_size("row"), lax.axis_size("col")
    peers = row_count * col_count
    per_device = channels // 2 // peers
    last = per_device // TAIL
    sizes = [per_device - last, last] if last else [per_device]
    rowh = halo(sky_cube, "row", 0)
    colh = halo(sky_cube, "col", 1)
    corner = halo(colh, "row", 0)
    brow = band_tables(tile_rows)
    bcol = band_tables(tile_cols).transpose(0, 2, 1)
    front = lambda x: x.transpose(2, 0, 1)
    masked, power = smooth(
        half_widths,
        front(sky_cube),
        front(rowh),
        front(colh),
        front(corner),
        pixel_mask.astype(jnp.float32),
        brow,
        bcol,
    )
    power_sum = lax.psum(jnp.sum(power, axis=1), ("row", "col"))
    weights = 1.0 / (power_sum / (NR * NC) + 1e-05)
    channel_weights = weights / jnp.mean(weights)
    weighted_modes = foreground_modes * weights[None, :]
    normal_matrix = jnp.dot(
        weighted_modes, foreground_modes.T, precision=highest, preferred_element_type=jnp.float32
    )
    factor = jnp.linalg.cholesky(normal_matrix)
    fit = jax.scipy.linalg.cho_solve((factor, True), weighted_modes)
    fit = jnp.concatenate(outer_split3(fit), axis=0)
    m1, m2, m3 = outer_split3(foreground_modes.T)
    modes = jnp.concatenate([m1, m1, m2, m2, m1, m3], axis=1)
    table = chunked_delay_table(channels, peers, sizes)
    pieces = clean_delay(masked, fit, modes, table, sizes, peers)
    ct, rt = dft_table(NC), dft_table(NR)
    ctab = jnp.concatenate(
        [jnp.concatenate([ct[0, 0], ct[1, 0]], axis=1), jnp.concatenate([ct[0, 1], ct[1, 1]], axis=1)], axis=0
    )
    rtab = jnp.concatenate(
        [jnp.concatenate([rt[0, 0], rt[0, 1]], axis=1), jnp.concatenate([rt[1, 0], rt[1, 1]], axis=1)], axis=0
    )

    spectrum = None
    first = 0
    for piece, size in zip(pieces, sizes):
        got = lax.all_to_all(piece, ("row", "col"), split_axis=0, concat_axis=0, tiled=True)
        spectrum = spatial(got, ctab, rtab, spectrum, first, per_device, row_count, col_count)
        first += size
    return (spectrum, channel_weights)


def pick_body(sky_cube, *rest):
    rows, cols, channels = sky_cube.shape
    fits = rows % 128 == 0 and cols % 128 == 0 and channels % 128 == 0
    return (tiled_body if fits else body)(sky_cube, *rest)


def solution(mesh):
    return jax.shard_map(
        pick_body,
        mesh=mesh,
        in_specs=(P(("grp", "row"), "col", None), P(), P(("grp", "row"), "col"), P("grp", None)),
        out_specs=(P(("grp", "row", "col"), None, None, None), P("grp")),
        check_vma=False,
    )
```

profile of v0, /device:TPU:0, one launch (start us, length us, event | category | flops | bytes accessed | tf_op | source)
XLA Modules:
  0.0 635.4 jit_solution(8528017725381119442)
XLA Ops:
  0.6 4.7 fusion.60
  5.4 3.7 collective-permute-start.2
  9.0 1.3 collective-permute-start.3
  10.3 23.7 %copy.28 = bf16[128,128,512]{1,0,2:T(8,128)(2,1)} copy(bf16[128,128,512]{2,1,0:T(8,128)(2,1)} %param.4) | data formatting | bytes 33554432 | tf_op args[0]
  34.1 5.1 fusion.61
  39.1 5.6 collective-permute-start
  44.7 1.3 collective-permute-start.1
  46.5 0.2 fusion.39
  47.0 1.3 fusion.7.bcol_ref
  48.3 1.5 fusion.2.brow_ref
  49.8 1.8 constant_dynamic-update-slice_fusion.1
  51.6 0.2 constant_dynamic-update-slice_fusion
  51.8 2.0 copy-done
  53.9 4.6 collective-permute-start.4
  58.5 1.3 collective-permute-start.5
  59.8 0.6 convert_element_type.104.mask_ref
  60.5 0.9 concatenate.45.modes_ref
  61.4 5.6 multiply_convert_fusion.1.table_ref
  67.1 23.1 %copy.31 = bf16[128,32,512]{1,0,2:T(8,128)(2,1)} copy(bf16[128,32,512]{2,1,0:T(8,128)(2,1)} %copy-done) | data formatting | bytes 8388608 | tf_op jit(solution)/shard_map/concatenate | solution.py:334
  90.2 5.3 collective-permute-done.1
  95.4 5.0 maximum_bitcast_fusion.rowh_ref
  100.5 0.3 collective-permute-done.4
  100.7 5.7 collective-permute-done.5
  106.5 6.5 %copy.32 = bf16[32,32,512]{1,0,2:T(8,128)(2,1)} copy(bf16[32,32,512]{2,1,0:T(8,128)(2,1)S(1)} %pad_maximum_fusion.4) | data formatting | bytes 2097152 | tf_op jit(solution)/shard_map/concatenate | solution.py:334
  113.0 46.1 %smooth.1 = (f32[128,512,128]{2,1,0:T(8,128)}, f32[512,128]{1,0:T(8,128)}) custom-call(s32[512]{0:T(512)} %hw_ref.1, bf16[512,128,128]{2,1,0:T(8,128)(2,1)} %bitcast.39, bf16[512,32,128]{2,1,0:T(8,128)(2,1)} %maximum_bitcast_fusion.rowh_ref, bf16[512,128,32]{2,1,0:T(8,128)(2,1)} %bitcast.40, bf16[512,32,32]{2,1,0:T(8,128)(2,1)} %bitcast.41, ...), custom_call_target="tpu_custom_call" | custom-call | tf_op jit(solution)/shard_map/smooth/pallas_call | solution.py:203
  159.1 1.1 reduce_sum.32
  160.2 29.5 %psum.7 = f32[512]{0:T(512)S(1)} all-reduce(f32[512]{0:T(512)S(1)} %reduce_sum.32), channel_id=1, replica_groups=mesh['grp'=2,'row'=4,'col'=4] {'row','col'}, use_global_device_ids=true, to_apply=%region_2.3 | all-reduce | flops 512 | bytes 4096 | tf_op jit(solution)/shard_map/psum | solution.py:375
  189.6 0.6 fusion.58
  190.5 1.5 cholesky.16
  192.0 0.7 compare_reduce_fusion
  192.7 0.6 fusion.34
  193.3 1.2 custom-call.10
  194.6 0.2 fusion.25
  194.8 0.2 reduce-precision_convert_fusion.3
  195.0 0.6 pad_maximum_fusion.5.fit_ref
  195.6 50.6 %clean_delay.1 = (bf16[16,28,128,128]{3,2,1,0:T(8,128)(2,1)}, bf16[16,4,128,128]{3,2,1,0:T(8,128)(2,1)}) custom-call(f32[128,512,128]{2,1,0:T(8,128)} %get-tuple-element.6.masked_ref, bf16[48,512]{1,0:T(8,128)(2,1)} %pad_maximum_fusion.5.fit_ref, bf16[512,96]{1,0:T(8,128)(2,1)} %concatenate.45.modes_ref, bf16[512,512]{1,0:T(8,128)(2,1)} %multiply_convert_fusion.1.table_ref), custom_call_target="tpu_custom_call" | custom-call | tf_op jit(solution)/shard_map/clean_delay/pallas_call | solution.py:270
  246.2 5.2 all-to-all-start.1
  251.4 4.0 fusion.20
  255.4 4.0 negate_convert_fusion
  259.4 251.9 %all-to-all-done.1.data_ref = bf16[16,28,128,128]{3,2,1,0:T(8,128)(2,1)} async-done(((bf16[16,28,128,128]{3,2,1,0:T(8,128)(2,1)}), bf16[16,28,128,128]{3,2,1,0:T(8,128)(2,1)}, u32[]{:S(2)}, u32[]{:S(2)}) %all-to-all-start.1) | async-done | bytes 14680096 | tf_op jit(solution)/shard_map/all_to_all | solution.py:400
  511.3 61.7 %all-to-all-start = ((bf16[16,4,128,128]{3,2,1,0:T(8,128)(2,1)}), bf16[16,4,128,128]{3,2,1,0:T(8,128)(2,1)S(1)}, u32[]{:S(2)}, u32[]{:S(2)}) async-start(bf16[16,4,128,128]{3,2,1,0:T(8,128)(2,1)} %get-tuple-element.8), calls=%async_computation | async-start | bytes 4194304 | tf_op jit(solution)/shard_map/all_to_all | solution.py:400
  573.1 4.0 multiply_convert_fusion
  577.0 0.2 maximum_bitcast_fusion.2
  577.4 10.1 %fusion.4 = (bf16[1024,1024]{1,0:T(8,128)(2,1)}, bf16[1024,1024]{1,0:T(8,128)(2,1)}) fusion(bf16[512,512]{1,0:T(8,128)(2,1)S(1)} %get-tuple-element.23, bf16[512,512]{1,0:T(8,128)(2,1)S(1)} %get-tuple-element.34, bf16[512,512]{1,0:T(8,128)(2,1)S(1)} %get-tuple-element.35, bf16[512,512]{1,0:T(8,128)(2,1)S(1)} %get-tuple-element.22), kind=kLoop, calls=%fused_computation.10 | loop fusion | flops 14680064 | bytes 6291456 | tf_op jit(solution)/shard_map/concatenate | solution.py:393
  588.1 0.6 multiply_divide_fusion
  588.7 36.9 %spatial.2.refs_0_ = f32[16,2,512,512]{3,2,1,0:T(8,128)} custom-call(bf16[16,28,128,128]{3,2,1,0:T(8,128)(2,1)} %all-to-all-done.1.data_ref, bf16[1024,1024]{1,0:T(8,128)(2,1)} %get-tuple-element.19.ctab_ref, bf16[1024,1024]{1,0:T(8,128)(2,1)} %get-tuple-element.18.rtab_ref), custom_call_target="tpu_custom_call" | custom-call | flops 30064771072 | bytes 44040192 | tf_op jit(solution)/shard_map/spatial/pallas_call | solution.py:311
  625.5 1.3 copy-done.1
  626.8 8.6 %spatial.3 = f32[16,2,512,512]{3,2,1,0:T(8,128)} custom-call(bf16[16,4,128,128]{3,2,1,0:T(8,128)(2,1)} %copy-done.1, bf16[1024,1024]{1,0:T(8,128)(2,1)} %get-tuple-element.19.ctab_ref, bf16[1024,1024]{1,0:T(8,128)(2,1)} %get-tuple-element.18.rtab_ref, f32[16,2,512,512]{3,2,1,0:T(8,128)} %spatial.2.refs_0_), custom_call_target="tpu_custom_call", output_to_operand_aliasing={{}: (3, {})} | custom-call | flops 4294967296 | bytes 6291456 | tf_op jit(solution)/shard_map/spatial/pallas_call | solution.py:311
  (35 shorter events, 1.3 us)
Async XLA Ops:
  5.4 44.4 %collective-permute-start.2 = (bf16[128,16,512]{2,1,0:T(8,128)(2,1)}, bf16[128,16,512]{2,1,0:T(8,128)(2,1)}, u32[]{:S(2)}, u32[]{:S(2)}) collective-permute-start(bf16[128,16,512]{2,1,0:T(8,128)(2,1)} %get-tuple-element.13), channel_id=1, source_target_pairs={{0,1},{1,2},{2,3},{4,5},{5,6},{6,7},{8,9},{9,10},{10,11},{12,13},{... | collective-permute-start | bytes 6291464 | tf_op jit(solution)/shard_map/ppermute | solution.py:332
  9.0 42.5 %collective-permute-start.3 = (bf16[128,16,512]{2,1,0:T(8,128)(2,1)}, bf16[128,16,512]{2,1,0:T(8,128)(2,1)S(1)}, u32[]{:S(2)}, u32[]{:S(2)}) collective-permute-start(bf16[128,16,512]{2,1,0:T(8,128)(2,1)} %get-tuple-element.12), channel_id=1, source_target_pairs={{1,0},{2,1},{3,2},{5,4},{6,5},{7,6},{9,8},{10,9},{11,10},{13,12},{... | collective-permute-start | bytes 6291464 | tf_op jit(solution)/shard_map/ppermute | solution.py:333
  34.0 12.3 %copy-start.2 = (f32[16,512]{1,0:T(8,128)S(1)}, f32[16,512]{1,0:T(8,128)}, u32[]{:S(2)}) copy-start(f32[16,512]{1,0:T(8,128)} %param.7) | copy-start | bytes 98308
  39.1 51.0 %collective-permute-start = (bf16[16,128,512]{1,0,2:T(8,128)(2,1)}, bf16[16,128,512]{1,0,2:T(8,128)(2,1)}, u32[]{:S(2)}, u32[]{:S(2)}) collective-permute-start(bf16[16,128,512]{1,0,2:T(8,128)(2,1)} %get-tuple-element.14), channel_id=1, source_target_pairs={{0,4},{4,8},{8,12},{1,5},{5,9},{9,13},{2,6},{6,10},{10,14},{3,7},{... | collective-permute-start | bytes 6291464 | tf_op jit(solution)/shard_map/ppermute | solution.py:332
  44.7 50.7 %collective-permute-start.1 = (bf16[16,128,512]{1,0,2:T(8,128)(2,1)}, bf16[16,128,512]{1,0,2:T(8,128)(2,1)}, u32[]{:S(2)}, u32[]{:S(2)}) collective-permute-start(bf16[16,128,512]{1,0,2:T(8,128)(2,1)} %get-tuple-element.15), channel_id=1, source_target_pairs={{4,0},{8,4},{12,8},{5,1},{9,5},{13,9},{6,2},{10,6},{14,10},{7,3},{... | collective-permute-start | bytes 6291464 | tf_op jit(solution)/shard_map/ppermute | solution.py:333
  51.8 2.0 copy-start
  53.8 6.0 copy-start.3
  53.9 46.8 %collective-permute-start.4 = (bf16[16,32,512]{2,1,0:T(8,128)(2,1)S(1)}, bf16[16,32,512]{2,1,0:T(8,128)(2,1)S(1)}, u32[]{:S(2)}, u32[]{:S(2)}) collective-permute-start(bf16[16,32,512]{2,1,0:T(8,128)(2,1)S(1)} %get-tuple-element.16), channel_id=1, source_target_pairs={{0,4},{4,8},{8,12},{1,5},{5,9},{9,13},{2,6},{6,10},{10,14},{3,7},{... | collective-permute-start | bytes 1572872 | tf_op jit(solution)/shard_map/ppermute | solution.py:332
  58.5 47.9 %collective-permute-start.5 = (bf16[16,32,512]{2,1,0:T(8,128)(2,1)S(1)}, bf16[16,32,512]{2,1,0:T(8,128)(2,1)S(1)}, u32[]{:S(2)}, u32[]{:S(2)}) collective-permute-start(bf16[16,32,512]{2,1,0:T(8,128)(2,1)S(1)} %get-tuple-element.17), channel_id=1, source_target_pairs={{4,0},{8,4},{12,8},{5,1},{9,5},{13,9},{6,2},{10,6},{14,10},{7,3},{... | collective-permute-start | bytes 1572872 | tf_op jit(solution)/shard_map/ppermute | solution.py:333
  246.2 265.1 %all-to-all-start.1 = ((bf16[16,28,128,128]{3,2,1,0:T(8,128)(2,1)}), bf16[16,28,128,128]{3,2,1,0:T(8,128)(2,1)}, u32[]{:S(2)}, u32[]{:S(2)}) async-start(bf16[16,28,128,128]{3,2,1,0:T(8,128)(2,1)} %get-tuple-element.9), calls=%async_computation.1 | async-start | bytes 29360128 | tf_op jit(solution)/shard_map/all_to_all | solution.py:400
  511.3 114.2 %all-to-all-start = ((bf16[16,4,128,128]{3,2,1,0:T(8,128)(2,1)}), bf16[16,4,128,128]{3,2,1,0:T(8,128)(2,1)S(1)}, u32[]{:S(2)}, u32[]{:S(2)}) async-start(bf16[16,4,128,128]{3,2,1,0:T(8,128)(2,1)} %get-tuple-element.8), calls=%async_computation | async-start | bytes 4194304 | tf_op jit(solution)/shard_map/all_to_all | solution.py:400
  625.5 1.3 copy-start.1
where the time goes:
time: 638 us; the launch traced here: 635 us
  waiting for transfers between devices  263 us (41%)
  Pallas kernels  142 us (22%)
  starting transfers between devices  84.7 us (13%)
  local copies, waits for them, and re-layouts  69.8 us (11%)
  other arithmetic  44.1 us (7%)
  blocking collectives  29.5 us (5%)
    all_to_all x2, waiting for transfers between devices, tiled_body(): lax.all_to_all(piece, ('row', 'col'), split_axis=0, concat_axis=0, tiled=...  252 us
    all_to_all x2, starting transfers between devices, tiled_body(): lax.all_to_all(piece, ('row', 'col'), split_axis=0, concat_axis=0, tiled=...  67 us
    pallas_call x1, Pallas kernels, clean_delay(): pl.pallas_call(functools.partial(delay_kernel, len(sizes)), grid=(rows //...  50.6 us
    pallas_call x1, Pallas kernels, smooth(): pl.pallas_call(smooth_kernel, grid_spec=pltpu.PrefetchScalarGridSpec(num_...  46.1 us
    pallas_call x2, Pallas kernels, spatial(): pl.pallas_call(functools.partial(spatial_kernel, row_count, col_count, le...  45.4 us
    concatenate x3, local copies, waits for them, and re-layouts, halo(): return jnp.concatenate([before, after], axis=dim)  29.8 us
    psum x1, blocking collectives, tiled_body(): power_sum = lax.psum(jnp.sum(power, axis=1), ('row', 'col'))  29.5 us
    unnamed x11, local copies, waits for them, and re-layouts  29 us
  transfers between devices with their start and end apart: 8, of which 4 were waited for; matrix products, arithmetic and copies ran while one was open for 15% of the time, Pallas kernels for 6%

commit v1 on v0

--- a/solution.py
+++ b/solution.py
@@ -154,6 +154,8 @@
 
 FBLOCK = 16
 RBLOCK = 16
+LANES = 128
+MESH = pl.DeviceIdType.MESH
 
 
 def band_tables(outputs):
@@ -180,15 +182,38 @@
     return (profile(t, w3, s3) / n3).astype(jnp.bfloat16)
 
 
-def smooth_kernel(hw_ref, main_ref, rowh_ref, colh_ref, corner_ref, mask_ref, brow_ref, bcol_ref, out_ref, pow_ref):
+def smooth_kernel(hw_ref, main_ref, rowh_ref, colh_ref, corner_ref, mask_ref, brow_ref, bcol_ref, out_ref, pow_ref, rows_t, cols_t):
     rows, fblock, cols = out_ref.shape
     flat = out_ref.reshape(rows * fblock, cols)
-    base = pl.program_id(0) * fblock
+    lanes = rowh_ref.shape[2]
+    pitch = lanes + 8
+    ring, side = rowh_ref.shape[0], colh_ref.shape[1]
+    packs = LANES // side
+    lines = (rows + ring) // packs
+    sub = pl.program_id(1) * fblock
+    base = pl.program_id(0) * lanes + sub
+
+    @pl.when(pl.program_id(1) == 0)
+    def _():
+        for ref, first in ((main_ref, 0), (rowh_ref, rows)):
+            def turn(r, carry):
+                start = pl.multiple_of((first + r) * pitch, 8)
+                rows_t[pl.ds(start, lanes), :] = ref[r].T.astype(jnp.float32)
+                return carry
+
+            lax.fori_loop(0, ref.shape[0], turn, 0, unroll=8)
+        for g in range(lines):
+            group = [g + lines * p for p in range(packs)]
+            group = [colh_ref[r] if r < rows else corner_ref[r - rows] for r in group]
+            cols_t[g * pitch : g * pitch + lanes, :] = jnp.concatenate(group, axis=0).T.astype(jnp.float32)
+
     mask = mask_ref[...]
     for i in range(fblock):
         pick = hw_ref[base + i] - 1
-        left = jnp.concatenate([main_ref[i], rowh_ref[i]], axis=0)
-        right = jnp.concatenate([colh_ref[i], corner_ref[i]], axis=0)
+        left = rows_t[pl.ds(sub + i, rows + ring, stride=pitch), :].astype(jnp.bfloat16)
+        packed = cols_t[pl.ds(sub + i, lines, stride=pitch), :]
+        right = [packed[:, side * p : side * (p + 1)] for p in range(packs)]
+        right = jnp.concatenate(right, axis=0).astype(jnp.bfloat16)
         ext = jnp.concatenate([left, right], axis=1)
         part = jnp.dot(brow_ref[pick], ext, preferred_element_type=jnp.float32).astype(jnp.bfloat16)
         done = jnp.dot(part, bcol_ref[pick], preferred_element_type=jnp.float32) * mask
@@ -197,18 +222,32 @@
 
 
 def smooth(half_widths, main, rowh, colh, corner, mask, brow, bcol):
-    channels, rows, cols = main.shape
-    step = lambda a: pl.BlockSpec((FBLOCK,) + a.shape[1:], lambda i, hw: (i, 0, 0))
-    whole = lambda a: pl.BlockSpec(a.shape, lambda i, hw: (0,) * a.ndim)
+    rows, cols, channels = main.shape
+    inner = LANES // FBLOCK
+    ring, side = rowh.shape[0], colh.shape[1]
+    raw = lambda a: pl.BlockSpec(a.shape[:2] + (LANES,), lambda i, j, hw: (0, 0, i))
+    whole = lambda a: pl.BlockSpec(a.shape, lambda i, j, hw: (0,) * a.ndim)
     return pl.pallas_call(
         smooth_kernel,
         grid_spec=pltpu.PrefetchScalarGridSpec(
             num_scalar_prefetch=1,
-            grid=(channels // FBLOCK,),
-            in_specs=[step(main), step(rowh), step(colh), step(corner), whole(mask), whole(brow), whole(bcol)],
+            grid=(channels // LANES, inner),
+            in_specs=[
+                raw(main),
+                raw(rowh),
+                raw(colh),
+                raw(corner),
+                whole(mask),
+                whole(brow),
+                whole(bcol),
+            ],
             out_specs=[
-                pl.BlockSpec((rows, FBLOCK, cols), lambda i, hw: (0, i, 0)),
-                pl.BlockSpec((FBLOCK, cols), lambda i, hw: (i, 0)),
+                pl.BlockSpec((rows, FBLOCK, cols), lambda i, j, hw: (0, i * inner + j, 0)),
+                pl.BlockSpec((FBLOCK, cols), lambda i, j, hw: (i * inner + j, 0)),
+            ],
+            scratch_shapes=[
+                pltpu.VMEM(((rows + ring) * (LANES + 8), cols), jnp.float32),
+                pltpu.VMEM(((rows + ring) * side // LANES * (LANES + 8), LANES), jnp.float32),
             ],
         ),
         out_shape=[
@@ -234,8 +273,8 @@
     return [v.astype(jnp.bfloat16) for v in (first, second, third)]
 
 
-def delay_kernel(n, masked_ref, fit_ref, modes_ref, table_ref, *refs):
-    outs, stage = refs[:n], refs[n]
+def delay_kernel(sizes, merged, masked_ref, fit_ref, modes_ref, table_ref, *refs):
+    outs, stage = refs[:-1], refs[-1]
     rblock, channels, cols = masked_ref.shape
     k = fit_ref.shape[0] // 3
     dot = functools.partial(jnp.dot, preferred_element_type=jnp.float32)
@@ -257,34 +296,127 @@
         return carry
 
     lax.fori_loop(0, rblock // 2, pair, 0, unroll=2)
-    start = 0
-    for out in outs:
-        size = math.prod(out.shape[:3])
-        out[...] = stage[start : start + size, :].astype(jnp.bfloat16).reshape(out.shape)
-        start += size
-
-
-def clean_delay(masked, fit, modes, table, sizes, peers):
-    rows, channels, cols = masked.shape
+    start, slot = 0, 0
+    for n, size in enumerate(sizes):
+        out = outs[0] if merged else outs[n]
+        peers = out.shape[0]
+        rows = peers * 2 * size * rblock
+        part = stage[start : start + rows, :].astype(jnp.bfloat16)
+        out[:, slot : slot + 2 * size] = part.reshape(peers, 2 * size, rblock, cols)
+        start += rows
+        slot += 2 * size if merged else 0
+
+
+def clean_delay(masked, fit, modes, table, sizes, peers, first, count, merged):
+    channels, cols = masked.shape[1:]
+    base = first // RBLOCK
     whole = lambda a: pl.BlockSpec(a.shape, lambda i: (0,) * a.ndim)
+    groups = [sum(sizes)] if merged else sizes
     return pl.pallas_call(
-        functools.partial(delay_kernel, len(sizes)),
-        grid=(rows // RBLOCK,),
-        in_specs=[pl.BlockSpec((RBLOCK, channels, cols), lambda i: (i, 0, 0)), whole(fit), whole(modes), whole(table)],
-        out_specs=[pl.BlockSpec((peers, 2 * k, RBLOCK, cols), lambda i: (0, 0, i, 0)) for k in sizes],
-        out_shape=[jax.ShapeDtypeStruct((peers, 2 * k, rows, cols), jnp.bfloat16) for k in sizes],
+        functools.partial(delay_kernel, sizes, merged),
+        grid=(count // RBLOCK,),
+        in_specs=[
+            pl.BlockSpec((RBLOCK, channels, cols), lambda i: (base + i, 0, 0)),
+            whole(fit),
+            whole(modes),
+            whole(table),
+        ],
+        out_specs=[pl.BlockSpec((peers, 2 * k, RBLOCK, cols), lambda i: (0, 0, i, 0)) for k in groups],
+        out_shape=[jax.ShapeDtypeStruct((peers, 2 * k, count, cols), jnp.bfloat16) for k in groups],
         scratch_shapes=[pltpu.VMEM((table.shape[0] * RBLOCK, cols), jnp.float32)],
+        cost_estimate=pl.CostEstimate(
+            flops=2 * count * cols * channels * (channels + 288),
+            bytes_accessed=count * cols * channels * 6,
+            transcendentals=0,
+        ),
         name="clean_delay",
     )(masked, fit, modes, table)
 
 
-def spatial_kernel(row_count, col_count, inputs, data_ref, ctab_ref, rtab_ref, *refs):
-    out_ref = refs[inputs - 3]
+def solve_kernel(row_count, col_count, pixels, power_ref, modes_ref, fit_ref, scale_ref, mine, gathered, send_sem, recv_sem):
+    grp, row, col = lax.axis_index("grp"), lax.axis_index("row"), lax.axis_index("col")
+    me = row * col_count + col
+    others = []
+    for k in range(1, row_count * col_count):
+        r = lax.rem(row + k // col_count, row_count)
+        c = lax.rem(col + k % col_count, col_count)
+        others.append((grp, r, c))
+    barrier = pltpu.get_barrier_semaphore()
+    for other in others:
+        pl.semaphore_signal(barrier, inc=1, device_id=other, device_id_type=MESH)
+    own = jnp.sum(jnp.transpose(power_ref[...]), axis=0, keepdims=True)
+    own = jnp.broadcast_to(own, mine.shape)
+    mine[...] = own
+    pl.semaphore_wait(barrier, len(others))
+    copies = []
+    for k, other in enumerate(others):
+        copies.append(
+            pltpu.make_async_remote_copy(
+                src_ref=mine,
+                dst_ref=gathered.at[me],
+                send_sem=send_sem.at[k],
+                recv_sem=recv_sem.at[k],
+                device_id=other,
+                device_id_type=MESH,
+            )
+        )
+    for copy in copies:
+        copy.start()
+    gathered[me] = own
+    modes = modes_ref[...]
+    for copy in copies:
+        copy.wait()
+    total = gathered[0]
+    for k in range(1, row_count * col_count):
+        total = total + gathered[k]
+    weights = (1.0 / (total / pixels + 1e-05))[:1]
+    channels = weights.shape[1]
+    scale_ref[...] = weights / (jnp.sum(weights, axis=1, keepdims=True) / channels)
+    fit = modes * weights
+    normal = lax.dot_general(
+        fit, modes, (((1,), (1,)), ((), ())), precision=highest, preferred_element_type=jnp.float32
+    )
+    line = lax.broadcasted_iota(jnp.int32, (modes.shape[0], 1), 0)
+    for k in range(modes.shape[0]):
+        inverse = 1.0 / normal[k : k + 1, k : k + 1]
+        factor = normal[:, k : k + 1]
+        top = normal[k : k + 1] * inverse
+        top_fit = fit[k : k + 1] * inverse
+        normal = jnp.where(line == k, top, normal - factor * top)
+        fit = jnp.where(line == k, top_fit, fit - factor * top_fit)
+    fit_ref[...] = jnp.concatenate(split3(fit), axis=0)
+
+
+def solve(power, modes, row_count, col_count):
+    channels = power.shape[0]
+    peers = row_count * col_count
+    return pl.pallas_call(
+        functools.partial(solve_kernel, row_count, col_count, NR * NC),
+        in_specs=[pl.BlockSpec(memory_space=pltpu.VMEM)] * 2,
+        out_specs=[pl.BlockSpec(memory_space=pltpu.VMEM)] * 2,
+        out_shape=[
+            jax.ShapeDtypeStruct((3 * modes.shape[0], channels), jnp.bfloat16),
+            jax.ShapeDtypeStruct((1, channels), jnp.float32),
+        ],
+        scratch_shapes=[
+            pltpu.VMEM((8, channels), jnp.float32),
+            pltpu.VMEM((peers, 8, channels), jnp.float32),
+            pltpu.SemaphoreType.DMA((peers - 1,)),
+            pltpu.SemaphoreType.DMA((peers - 1,)),
+        ],
+        compiler_params=pltpu.CompilerParams(collective_id=0, has_side_effects=True),
+        name="solve",
+    )(power, modes)
+
+
+def spatial_kernel(row_count, col_count, inputs, head_ref, data_ref, ctab_ref, rtab_ref, *refs):
+    out_ref = refs[inputs - 4]
     nr, nc = out_ref.shape[2:]
     lines = []
     for i in range(row_count):
-        tiles = [data_ref[i * col_count + j, m] for m in range(2) for j in range(col_count)]
-        lines.append(jnp.concatenate(tiles, axis=1))
+        for ref in (head_ref, data_ref):
+            tiles = [ref[i * col_count + j, m] for m in range(2) for j in range(col_count)]
+            lines.append(jnp.concatenate(tiles, axis=1))
     slab = jnp.concatenate(lines, axis=0)
     half = jnp.dot(slab, ctab_ref[...], preferred_element_type=jnp.float32).astype(jnp.bfloat16)
     half = jnp.concatenate([half[:, :nc], half[:, nc:]], axis=0)
@@ -294,15 +426,20 @@
         )
 
 
-def spatial(data, ctab, rtab, before, first, total, row_count, col_count):
+def spatial(head, data, ctab, rtab, before, first, total, row_count, col_count):
     peers, slots, rows, cols = data.shape
     items = slots // 2
     whole = lambda a: pl.BlockSpec(a.shape, lambda i: (0,) * a.ndim)
     nr, nc = rtab.shape[0] // 2, ctab.shape[0] // 2
-    in_specs = [pl.BlockSpec((peers, 2, rows, cols), lambda i: (0, i, 0, 0)), whole(ctab), whole(rtab)]
+    in_specs = [
+        pl.BlockSpec((peers, 2) + head.shape[2:], lambda i: (0, first + i, 0, 0)),
+        pl.BlockSpec((peers, 2, rows, cols), lambda i: (0, i, 0, 0)),
+        whole(ctab),
+        whole(rtab),
+    ]
     out_specs = [pl.BlockSpec((1, 2, nr, nc), lambda i: (first + i, 0, 0, 0))]
     out_shape = [jax.ShapeDtypeStruct((total, 2, nr, nc), jnp.float32)]
-    args = [data, ctab, rtab]
+    args = [head, data, ctab, rtab]
     alias = {}
     if before is not None:
         alias[len(args)] = 0
@@ -358,34 +495,28 @@
     sizes = [per_device - last, last] if last else [per_device]
     rowh = halo(sky_cube, "row", 0)
     colh = halo(sky_cube, "col", 1)
-    corner = halo(colh, "row", 0)
+    corner = halo(rowh, "col", 1)
     brow = band_tables(tile_rows)
     bcol = band_tables(tile_cols).transpose(0, 2, 1)
-    front = lambda x: x.transpose(2, 0, 1)
     masked, power = smooth(
         half_widths,
-        front(sky_cube),
-        front(rowh),
-        front(colh),
-        front(corner),
+        sky_cube,
+        rowh,
+        colh,
+        corner,
         pixel_mask.astype(jnp.float32),
         brow,
         bcol,
     )
-    power_sum = lax.psum(jnp.sum(power, axis=1), ("row", "col"))
-    weights = 1.0 / (power_sum / (NR * NC) + 1e-05)
-    channel_weights = weights / jnp.mean(weights)
-    weighted_modes = foreground_modes * weights[None, :]
-    normal_matrix = jnp.dot(
-        weighted_modes, foreground_modes.T, precision=highest, preferred_element_type=jnp.float32
-    )
-    factor = jnp.linalg.cholesky(normal_matrix)
-    fit = jax.scipy.linalg.cho_solve((factor, True), weighted_modes)
-    fit = jnp.concatenate(outer_split3(fit), axis=0)
+    fit, channel_weights = solve(power, foreground_modes, row_count, col_count)
+    channel_weights = channel_weights.reshape(channels)
     m1, m2, m3 = outer_split3(foreground_modes.T)
     modes = jnp.concatenate([m1, m1, m2, m2, m1, m3], axis=1)
     table = chunked_delay_table(channels, peers, sizes)
-    pieces = clean_delay(masked, fit, modes, table, sizes, peers)
+    exchange = lambda x: lax.all_to_all(x, ("row", "col"), split_axis=0, concat_axis=0, tiled=True)
+    (head,) = clean_delay(masked, fit, modes, table, sizes, peers, 0, RBLOCK, True)
+    pieces = clean_delay(masked, fit, modes, table, sizes, peers, RBLOCK, tile_rows - RBLOCK, False)
+    head = exchange(head)
     ct, rt = dft_table(NC), dft_table(NR)
     ctab = jnp.concatenate(
         [jnp.concatenate([ct[0, 0], ct[1, 0]], axis=1), jnp.concatenate([ct[0, 1], ct[1, 1]], axis=1)], axis=0
@@ -397,8 +528,7 @@
     spectrum = None
     first = 0
     for piece, size in zip(pieces, sizes):
-        got = lax.all_to_all(piece, ("row", "col"), split_axis=0, concat_axis=0, tiled=True)
-        spectrum = spatial(got, ctab, rtab, spectrum, first, per_device, row_count, col_count)
+        spectrum = spatial(head, exchange(piece), ctab, rtab, spectrum, first, per_device, row_count, col_count)
         first += size
     return (spectrum, channel_weights)
 

time: 638 us -> 565 us (0.89)
  local copies, waits for them, and re-layouts: 69.8 us -> 19 us
  Pallas kernels: 142 us -> 177 us
  blocking collectives: 29.5 us -> 0 us
  waiting for transfers between devices: 263 us -> 246 us
    all_to_all x2 -> x3, waiting for transfers between devices: 252 us -> 215 us  [tiled_body(): lax.all_to_all(x, ('row', 'col'), split_axis=0, concat_axis=0, tiled=True)]
    ppermute x3, waiting for transfers between devices: 0.27 us -> 31.3 us  [halo(): lax.ppermute(lax.slice_in_dim(x, length - HALF, length, axis=dim), axis, up)]
    concatenate x3 -> x1, local copies, waits for them, and re-layouts: 29.8 us -> 0.2 us  [halo(): return jnp.concatenate([before, after], axis=dim)]
    psum x1 -> x0, blocking collectives: 29.5 us -> none  [tiled_body(): power_sum = lax.psum(jnp.sum(power, axis=1), ('row', 'col'))]
    unnamed x11 -> x15, local copies, waits for them, and re-layouts: 29 us -> 7 us
    pallas_call x1 -> x3, Pallas kernels: 50.6 us -> 72 us  [the longest x2 54.3 us: clean_delay(): pl.pallas_call(functools.partial(delay_kernel, sizes, merged), grid=(coun...]
    pallas_call x1, Pallas kernels: 46.1 us -> 59.1 us  [smooth(): pl.pallas_call(smooth_kernel, grid_spec=pltpu.PrefetchScalarGridSpec(num_...]
    ppermute x3, waiting for transfers between devices: 11 us -> 0.01 us  [halo(): after = lax.ppermute(lax.slice_in_dim(x, 0, HALF, axis=dim), axis, down)]
  transfers between devices with their start and end apart: 8 -> 9, of which waited for: 4 -> 2; matrix products, arithmetic and copies ran while one was open for 15% -> 8% of each run, Pallas kernels for 6% -> 14%
where the time goes in v1:
time: 565 us
  waiting for transfers between devices  246 us (44%)
  Pallas kernels  177 us (31%)
  starting transfers between devices  82.7 us (15%)
  other arithmetic  39 us (7%)
  local copies, waits for them, and re-layouts  19 us (3%)
    all_to_all x3, waiting for transfers between devices, tiled_body(): lax.all_to_all(x, ('row', 'col'), split_axis=0, concat_axis=0, tiled=True)  215 us
    all_to_all x3, starting transfers between devices, tiled_body(): lax.all_to_all(x, ('row', 'col'), split_axis=0, concat_axis=0, tiled=True)  67.8 us
    pallas_call x1, Pallas kernels, smooth(): pl.pallas_call(smooth_kernel, grid_spec=pltpu.PrefetchScalarGridSpec(num_...  59.1 us
    pallas_call x2, Pallas kernels, clean_delay(): pl.pallas_call(functools.partial(delay_kernel, sizes, merged), grid=(coun...  54.3 us
    pallas_call x2, Pallas kernels, spatial(): pl.pallas_call(functools.partial(spatial_kernel, row_count, col_count, le...  45.6 us
    ppermute x3, waiting for transfers between devices, halo(): lax.ppermute(lax.slice_in_dim(x, length - HALF, length, axis=dim), axis, up)  31.3 us
    pallas_call x1, Pallas kernels, solve(): pl.pallas_call(functools.partial(solve_kernel, row_count, col_count, NR *...  17.7 us
    another operation x3, other arithmetic  12 us
  transfers between devices with their start and end apart: 9, of which 2 were waited for; matrix products, arithmetic and copies ran while one was open for 8% of the time, Pallas kernels for 14%

profile of v1, /device:TPU:0, one launch (start us, length us, event | category | flops | bytes accessed | tf_op | source)
XLA Modules:
  0.0 564.6 jit_solution(14118313172523982675)
XLA Ops:
  0.6 4.7 fusion.45
  5.3 1.3 collective-permute-start.1
  6.6 0.0 copy-start.3
  6.6 6.9 %collective-permute-start = (bf16[16,128,512]{2,1,0:T(8,128)(2,1)}, bf16[16,128,512]{2,1,0:T(8,128)(2,1)}, u32[]{:S(2)}, u32[]{:S(2)}) collective-permute-start(bf16[16,128,512]{2,1,0:T(8,128)(2,1)} %get-tuple-element.17), channel_id=1, source_target_pairs={{0,4},{4,8},{8,12},{1,5},{5,9},{9,13},{2,6},{6,10},{10,14},{3,7},{... | collective-permute-start | bytes 6291464 | tf_op jit(solution)/shard_map/ppermute | solution.py:469
  13.5 4.7 fusion.44
  18.2 2.8 collective-permute-start.2
  21.0 1.3 collective-permute-start.3
  22.4 0.1 subtract_multiply_fusion
  22.4 0.1 pad_add_fusion.1
  22.5 0.1 negate_multiply_fusion.2
  22.6 0.1 copy.9
  22.8 0.2 fusion.26
  23.0 0.1 pad_add_fusion
  23.0 0.1 fusion.24
  23.2 0.1 fusion.22
  23.3 1.2 fusion.7.bcol_ref
  24.5 1.6 fusion.2.brow_ref
  26.1 31.3 %collective-permute-done = bf16[16,128,512]{2,1,0:T(8,128)(2,1)} collective-permute-done((bf16[16,128,512]{2,1,0:T(8,128)(2,1)}, bf16[16,128,512]{2,1,0:T(8,128)(2,1)}, u32[]{:S(2)}, u32[]{:S(2)}) %collective-permute-start) | collective-permute-done | bytes 2097184 | tf_op jit(solution)/shard_map/ppermute | solution.py:469
  57.4 1.8 constant_dynamic-update-slice_fusion.1
  59.2 0.2 constant_dynamic-update-slice_fusion.rowh_ref
  59.4 1.9 copy-done
  61.3 0.1 fusion.46
  61.4 1.3 collective-permute-start.4
  62.8 1.3 collective-permute-start.5
  64.1 0.6 convert_element_type.95.mask_ref
  64.7 1.0 concatenate.41.modes_ref
  65.7 5.6 multiply_convert_fusion.1.table_ref
  71.3 4.8 pad_maximum_fusion.colh_ref
  76.1 1.2 pad_maximum_fusion.5.corner_ref
  77.3 59.1 %smooth.1 = (f32[128,512,128]{2,1,0:T(8,128)}, f32[512,128]{1,0:T(8,128)}) custom-call(s32[512]{0:T(512)} %hw_ref.1, bf16[128,128,512]{2,1,0:T(8,128)(2,1)} %main_ref.1, bf16[32,128,512]{2,1,0:T(8,128)(2,1)} %copy-done, bf16[128,32,512]{2,1,0:T(8,128)(2,1)} %pad_maximum_fusion.colh_ref, bf16[32,32,512]{2,1,0:T(8,128)(2,1)} %pad_maximum_fusion.5.corner_ref, ...), custom_call_target="tpu_custom_call" | custom-call | tf_op jit(solution)/shard_map/smooth/pallas_call | solution.py:230
  136.4 17.7 %solve.1 = (bf16[48,512]{1,0:T(8,128)(2,1)}, f32[1,512]{1,0:T(1,128)}) custom-call(f32[512,128]{1,0:T(8,128)} %get-tuple-element.9.power_ref, f32[16,512]{1,0:T(8,128)} %modes_ref.1), custom_call_target="tpu_custom_call" | custom-call | tf_op jit(solution)/shard_map/solve/pallas_call | solution.py:393
  154.1 9.5 %clean_delay.2 = bf16[16,32,16,128]{3,2,1,0:T(8,128)(2,1)} custom-call(f32[128,512,128]{2,1,0:T(8,128)} %get-tuple-element.8.masked_ref, bf16[48,512]{1,0:T(8,128)(2,1)} %get-tuple-element.10.fit_ref, bf16[512,96]{1,0:T(8,128)(2,1)} %concatenate.41.modes_ref, bf16[512,512]{1,0:T(8,128)(2,1)} %multiply_convert_fusion.1.table_ref), custom_call_target="tpu_custom_call" | custom-call | flops 1677721600 | bytes 6291456 | tf_op jit(solution)/shard_map/clean_delay/pallas_call | solution.py:315
  163.6 5.9 %all-to-all-start = ((bf16[16,32,16,128]{3,2,1,0:T(8,128)(2,1)}), bf16[16,32,16,128]{3,2,1,0:T(8,128)(2,1)S(1)}, u32[]{:S(2)}, u32[]{:S(2)}) async-start(bf16[16,32,16,128]{3,2,1,0:T(8,128)(2,1)} %clean_delay.2), calls=%async_computation | async-start | bytes 4194304 | tf_op jit(solution)/shard_map/all_to_all | solution.py:516
  169.6 44.8 %clean_delay.3 = (bf16[16,28,112,128]{3,2,1,0:T(8,128)(2,1)}, bf16[16,4,112,128]{3,2,1,0:T(8,128)(2,1)}) custom-call(f32[128,512,128]{2,1,0:T(8,128)} %get-tuple-element.8.masked_ref, bf16[48,512]{1,0:T(8,128)(2,1)} %get-tuple-element.10.fit_ref, bf16[512,96]{1,0:T(8,128)(2,1)} %concatenate.41.modes_ref, bf16[512,512]{1,0:T(8,128)(2,1)} %multiply_convert_fusion.1.table_ref), custom_call_target="tpu_custom_call" | custom-call | flops 11744051200 | bytes 44040192 | tf_op jit(solution)/shard_map/clean_delay/pallas_call | solution.py:315
  214.4 1.3 copy-done.1
  215.7 7.5 %all-to-all-start.2 = ((bf16[16,28,112,128]{3,2,1,0:T(8,128)(2,1)}), bf16[16,28,112,128]{3,2,1,0:T(8,128)(2,1)}, u32[]{:S(2)}, u32[]{:S(2)}) async-start(bf16[16,28,112,128]{3,2,1,0:T(8,128)(2,1)} %get-tuple-element.12), calls=%async_computation.2 | async-start | bytes 25690112 | tf_op jit(solution)/shard_map/all_to_all | solution.py:516
  223.2 4.0 fusion.20
  227.2 4.0 multiply_convert_fusion
  231.1 4.0 negate_convert_fusion
  235.1 1.2 maximum_bitcast_fusion.1
  236.3 215.0 %all-to-all-done.2.data_ref = bf16[16,28,112,128]{3,2,1,0:T(8,128)(2,1)} async-done(((bf16[16,28,112,128]{3,2,1,0:T(8,128)(2,1)}), bf16[16,28,112,128]{3,2,1,0:T(8,128)(2,1)}, u32[]{:S(2)}, u32[]{:S(2)}) %all-to-all-start.2) | async-done | bytes 12845088 | tf_op jit(solution)/shard_map/all_to_all | solution.py:516
  451.3 54.4 %all-to-all-start.1 = ((bf16[16,4,112,128]{3,2,1,0:T(8,128)(2,1)}), bf16[16,4,112,128]{3,2,1,0:T(8,128)(2,1)S(1)}, u32[]{:S(2)}, u32[]{:S(2)}) async-start(bf16[16,4,112,128]{3,2,1,0:T(8,128)(2,1)} %get-tuple-element.11), calls=%async_computation.1 | async-start | bytes 3670016 | tf_op jit(solution)/shard_map/all_to_all | solution.py:516
  505.7 1.3 slice_bitcast_fusion.1
  507.1 10.1 %fusion.4 = (bf16[1024,1024]{1,0:T(8,128)(2,1)}, bf16[1024,1024]{1,0:T(8,128)(2,1)}) fusion(bf16[512,512]{1,0:T(8,128)(2,1)S(1)} %get-tuple-element.25, bf16[512,512]{1,0:T(8,128)(2,1)S(1)} %get-tuple-element.33, bf16[512,512]{1,0:T(8,128)(2,1)S(1)} %get-tuple-element.34, bf16[512,512]{1,0:T(8,128)(2,1)S(1)} %get-tuple-element.24), kind=kLoop, calls=%fused_computation.10 | loop fusion | flops 14680064 | bytes 6291456 | tf_op jit(solution)/shard_map/concatenate | solution.py:524
  517.2 37.0 %spatial.2.refs_0_ = f32[16,2,512,512]{3,2,1,0:T(8,128)} custom-call(bf16[16,32,16,128]{3,2,1,0:T(8,128)(2,1)} %copy-done.1, bf16[16,28,112,128]{3,2,1,0:T(8,128)(2,1)} %all-to-all-done.2.data_ref, bf16[1024,1024]{1,0:T(8,128)(2,1)} %get-tuple-element.21.ctab_ref, bf16[1024,1024]{1,0:T(8,128)(2,1)} %get-tuple-element.20.rtab_ref), custom_call_target="tpu_custom_call" | custom-call | flops 30064771072 | bytes 44040192 | tf_op jit(solution)/shard_map/spatial/pallas_call | solution.py:448
  554.2 1.2 copy-done.2
  555.4 8.6 %spatial.3 = f32[16,2,512,512]{3,2,1,0:T(8,128)} custom-call(bf16[16,32,16,128]{3,2,1,0:T(8,128)(2,1)} %copy-done.1, bf16[16,4,112,128]{3,2,1,0:T(8,128)(2,1)} %copy-done.2, bf16[1024,1024]{1,0:T(8,128)(2,1)} %get-tuple-element.21.ctab_ref, bf16[1024,1024]{1,0:T(8,128)(2,1)} %get-tuple-element.20.rtab_ref, ...), custom_call_target="tpu_custom_call", output_to_operand_aliasing={{}: (4, {})} | custom-call | flops 4294967296 | bytes 6291456 | tf_op jit(solution)/shard_map/spatial/pallas_call | solution.py:448
  564.0 0.6 copy.13
  (26 shorter events, 0.1 us)
Async XLA Ops:
  5.3 53.9 %collective-permute-start.1 = (bf16[16,128,512]{2,1,0:T(8,128)(2,1)}, bf16[16,128,512]{2,1,0:T(8,128)(2,1)S(1)}, u32[]{:S(2)}, u32[]{:S(2)}) collective-permute-start(bf16[16,128,512]{2,1,0:T(8,128)(2,1)} %get-tuple-element.16), channel_id=1, source_target_pairs={{4,0},{8,4},{12,8},{5,1},{9,5},{13,9},{6,2},{10,6},{14,10},{7,3},{... | collective-permute-start | bytes 6291464 | tf_op jit(solution)/shard_map/ppermute | solution.py:470
  6.6 16.0 %copy-start.3 = (f32[16,512]{1,0:T(8,128)S(1)}, f32[16,512]{1,0:T(8,128)}, u32[]{:S(2)}) copy-start(f32[16,512]{1,0:T(8,128)} %modes_ref.1) | copy-start | bytes 98308
  6.6 50.8 %collective-permute-start = (bf16[16,128,512]{2,1,0:T(8,128)(2,1)}, bf16[16,128,512]{2,1,0:T(8,128)(2,1)}, u32[]{:S(2)}, u32[]{:S(2)}) collective-permute-start(bf16[16,128,512]{2,1,0:T(8,128)(2,1)} %get-tuple-element.17), channel_id=1, source_target_pairs={{0,4},{4,8},{8,12},{1,5},{5,9},{9,13},{2,6},{6,10},{10,14},{3,7},{... | collective-permute-start | bytes 6291464 | tf_op jit(solution)/shard_map/ppermute | solution.py:469
  18.2 53.1 %collective-permute-start.2 = (bf16[128,16,512]{2,1,0:T(8,128)(2,1)}, bf16[128,16,512]{2,1,0:T(8,128)(2,1)}, u32[]{:S(2)}, u32[]{:S(2)}) collective-permute-start(bf16[128,16,512]{2,1,0:T(8,128)(2,1)} %get-tuple-element.14), channel_id=1, source_target_pairs={{0,1},{1,2},{2,3},{4,5},{5,6},{6,7},{8,9},{9,10},{10,11},{12,13},{... | collective-permute-start | bytes 6291464 | tf_op jit(solution)/shard_map/ppermute | solution.py:469
  21.0 50.3 %collective-permute-start.3 = (bf16[128,16,512]{2,1,0:T(8,128)(2,1)}, bf16[128,16,512]{2,1,0:T(8,128)(2,1)}, u32[]{:S(2)}, u32[]{:S(2)}) collective-permute-start(bf16[128,16,512]{2,1,0:T(8,128)(2,1)} %get-tuple-element.15), channel_id=1, source_target_pairs={{1,0},{2,1},{3,2},{5,4},{6,5},{7,6},{9,8},{10,9},{11,10},{13,12},{... | collective-permute-start | bytes 6291464 | tf_op jit(solution)/shard_map/ppermute | solution.py:470
  59.4 1.9 copy-start
  61.3 2.7 copy-start.4
  61.4 14.7 %collective-permute-start.4 = (bf16[32,16,512]{2,1,0:T(8,128)(2,1)S(1)}, bf16[32,16,512]{2,1,0:T(8,128)(2,1)S(1)}, u32[]{:S(2)}, u32[]{:S(2)}) collective-permute-start(bf16[32,16,512]{2,1,0:T(8,128)(2,1)S(1)} %get-tuple-element.18), channel_id=1, source_target_pairs={{0,1},{1,2},{2,3},{4,5},{5,6},{6,7},{8,9},{9,10},{10,11},{12,13},{... | collective-permute-start | bytes 1572872 | tf_op jit(solution)/shard_map/ppermute | solution.py:469
  62.8 13.3 %collective-permute-start.5 = (bf16[32,16,512]{2,1,0:T(8,128)(2,1)S(1)}, bf16[32,16,512]{2,1,0:T(8,128)(2,1)S(1)}, u32[]{:S(2)}, u32[]{:S(2)}) collective-permute-start(bf16[32,16,512]{2,1,0:T(8,128)(2,1)S(1)} %get-tuple-element.19), channel_id=1, source_target_pairs={{1,0},{2,1},{3,2},{5,4},{6,5},{7,6},{9,8},{10,9},{11,10},{13,12},{... | collective-permute-start | bytes 1572872 | tf_op jit(solution)/shard_map/ppermute | solution.py:470
  163.6 50.7 %all-to-all-start = ((bf16[16,32,16,128]{3,2,1,0:T(8,128)(2,1)}), bf16[16,32,16,128]{3,2,1,0:T(8,128)(2,1)S(1)}, u32[]{:S(2)}, u32[]{:S(2)}) async-start(bf16[16,32,16,128]{3,2,1,0:T(8,128)(2,1)} %clean_delay.2), calls=%async_computation | async-start | bytes 4194304 | tf_op jit(solution)/shard_map/all_to_all | solution.py:516
  214.4 1.3 copy-start.1
  215.7 235.6 %all-to-all-start.2 = ((bf16[16,28,112,128]{3,2,1,0:T(8,128)(2,1)}), bf16[16,28,112,128]{3,2,1,0:T(8,128)(2,1)}, u32[]{:S(2)}, u32[]{:S(2)}) async-start(bf16[16,28,112,128]{3,2,1,0:T(8,128)(2,1)} %get-tuple-element.12), calls=%async_computation.2 | async-start | bytes 25690112 | tf_op jit(solution)/shard_map/all_to_all | solution.py:516
  451.3 102.8 %all-to-all-start.1 = ((bf16[16,4,112,128]{3,2,1,0:T(8,128)(2,1)}), bf16[16,4,112,128]{3,2,1,0:T(8,128)(2,1)S(1)}, u32[]{:S(2)}, u32[]{:S(2)}) async-start(bf16[16,4,112,128]{3,2,1,0:T(8,128)(2,1)} %get-tuple-element.11), calls=%async_computation.1 | async-start | bytes 3670016 | tf_op jit(solution)/shard_map/all_to_all | solution.py:516
  554.1 9.9 %copy-start.5 = (f32[1,512]{1,0:T(1,128)S(1)}, f32[1,512]{1,0:T(1,128)}, u32[]{:S(2)}) copy-start(f32[1,512]{1,0:T(1,128)} %get-tuple-element.13) | copy-start | bytes 6148
  554.1 1.3 copy-start.2
